TPU v7x, 32 devices: a whole 2x2x4 slice. The times are simulated.
32 devices in a mesh: ctx: 2 (over x), tok: 8 (over z, core), head: 2 (over y).
Axes of the slice: x: 2, y: 2, z: 4, core: 2. Of those that a mesh axis runs over, the one named last changes fastest.
Arguments:
- keys: bfloat16 [2, 2, 4, 6144, 256], P(None, 'ctx', 'head', 'tok'), may hold values from -6 to 6
- values: bfloat16 [2, 2, 4, 6144, 256], P(None, 'ctx', 'head', 'tok'), may hold values from -6 to 6
- queries: bfloat16 [2, 2, 4, 6144, 256], P(None, 'ctx', 'head', 'tok'), may hold values from -6 to 6
- rates: float32 [2, 2, 4, 6144], P(None, 'ctx', 'head', 'tok'), may hold values from 0.1 to 3, as said below
- state_in: bfloat16 [2, 4, 3, 256, 512], P('ctx', 'head'), may hold values from -0.375 to 0.375
- fresh: bfloat16 [4, 3, 256, 512], P('head'), may hold values from -0.375 to 0.375
Outputs:
- outputs: bfloat16 [2, 2, 4, 6144, 256], P(None, 'ctx', 'head', 'tok')
Inputs may be any that keep to these rules, and one draw needn't show every extreme that they name: Positive per-token learning rates.
All inputs are finite; a program needn't handle non-finite values.
Results may differ from a plain program's by a relative error of at most 0.023.
Values may be sent and summed in bfloat16 or wider, within the bound.
No kernel may reach another device: no remote copies, remote signals or barrier semaphores. Data moves between devices by JAX's collectives and lax.ppermute only.
A program may use at most 64 MiB of HBM per device.

v0:
```python
import jax
import jax.numpy as jnp
from jax import lax
from jax.sharding import PartitionSpec as P


def from_behind(value, axis, steps):
    count = lax.axis_size(axis)
    first, last = (max(0, -steps), min(count, count - steps))
    return lax.ppermute(value, axis, [(source, source + steps) for source in range(first, last)])


def partial_grads(state, keys_p, values_p, rate_p):
    h_one = jnp.dot(keys_p, state[0], preferred_element_type=jnp.float32)
    h_three = jnp.dot(keys_p, state[1], preferred_element_type=jnp.float32)
    sig = jax.nn.sigmoid(h_one)
    act = (h_one * sig * h_three).astype(jnp.bfloat16)
    weighted = (rate_p[:, None] * values_p.astype(jnp.float32)).astype(jnp.bfloat16)
    dact = -jnp.dot(weighted, state[2], preferred_element_type=jnp.float32)
    d_one = (dact * h_three * sig * (1.0 + h_one * (1.0 - sig))).astype(jnp.bfloat16)
    d_three = (dact * h_one * sig).astype(jnp.bfloat16)
    contract = (((0,), (0,)), ((), ()))
    g_one = lax.dot_general(keys_p, d_one, contract, preferred_element_type=jnp.float32)
    g_three = lax.dot_general(keys_p, d_three, contract, preferred_element_type=jnp.float32)
    g_back = -lax.dot_general(weighted, act, contract, preferred_element_type=jnp.float32)
    return jnp.stack([g_one, g_three, g_back])


def apply_state(state, queries_h):
    p_one = jnp.dot(queries_h, state[0], preferred_element_type=jnp.float32)
    p_three = jnp.dot(queries_h, state[1], preferred_element_type=jnp.float32)
    mixed = (jax.nn.silu(p_one) * p_three).astype(jnp.bfloat16)
    contract = (((1,), (1,)), ((), ()))
    return lax.dot_general(mixed, state[2], contract, preferred_element_type=jnp.float32).astype(
        jnp.bfloat16
    )


def renormed(older_bf, grads, total_sq, heads_all, hidden):
    scale = 0.5 * jnp.sqrt(jnp.float32(3 * hidden * heads_all)) / jnp.sqrt(total_sq + 1e-06)
    older = older_bf.astype(jnp.float32)
    moved = older - scale * grads
    old_norm = jnp.sqrt(jnp.sum(older * older, axis=-2, keepdims=True))
    new_norm = jnp.sqrt(jnp.sum(moved * moved, axis=-2, keepdims=True) + 1e-06)
    return (moved * old_norm / new_norm).astype(jnp.bfloat16)


def block_tick(state, keys_t, values_t, rates_t, queries_t):
    heads_all = lax.axis_size("head") * state.shape[0]
    hidden = state.shape[3]
    grads = jax.vmap(partial_grads)(state, keys_t, values_t, rates_t)
    summed = lax.psum(grads.astype(jnp.bfloat16), "tok").astype(jnp.float32)
    total_sq = lax.psum(jnp.sum(summed * summed), "head")
    newer = renormed(state, summed, total_sq, heads_all, hidden)
    applied = jax.vmap(apply_state)(newer, queries_t)
    return (newer, applied)


def shards(keys, values, queries, rates, state_in, fresh):
    first_state, first_out = block_tick(
        state_in[0], keys[0, 0], values[0, 0], rates[0, 0], queries[0, 0]
    )
    arrived = from_behind(first_state, "ctx", 1)
    incoming = jnp.where(lax.axis_index("ctx") == 0, fresh, arrived)
    second_state, second_out = block_tick(
        incoming, keys[1, 0], values[1, 0], rates[1, 0], queries[1, 0]
    )
    return jnp.stack([first_out, second_out])[:, None]


def solution(mesh):
    in_specs = (
        P(None, "ctx", "head", "tok", None),
        P(None, "ctx", "head", "tok", None),
        P(None, "ctx", "head", "tok", None),
        P(None, "ctx", "head", "tok"),
        P("ctx", "head", None, None, None),
        P("head", None, None, None),
    )
    out_specs = P(None, "ctx", "head", "tok", None)
    return jax.shard_map(shards, mesh=mesh, in_specs=in_specs, out_specs=out_specs, check_vma=False)
```

profile of v0, /device:TPU:0, one launch (start us, length us, event | category | flops | bytes accessed | tf_op | source)
XLA Modules:
  0.0 232.4 jit_solution(3632334294932788770)
XLA Ops:
  6.5 1.6 copy.54
  9.7 0.7 copy-done.6
  10.4 0.6 fusion.91
  11.0 1.4 fusion.63
  12.5 1.6 fusion.52
  14.0 1.2 fusion.56
  15.3 1.3 maximum_bitcast_fusion
  16.6 64.7 %all-reduce.3.cloned.1.call-done = bf16[2,3,256,512]{3,2,0,1:T(8,128)(2,1)} async-done(((bf16[2,3,256,512]{3,2,0,1:T(8,128)(2,1)}), bf16[2,3,256,512]{3,2,0,1:T(8,128)(2,1)}) %all-reduce.3.cloned.1.call-update) | async-done | bytes 1572880 | tf_op jit(solution)/shard_map/psum | solution.py:52
  81.3 2.9 %fusion.1 = f32[]{:T(128)} fusion(bf16[2,3,256,512]{3,2,0,1:T(8,128)(2,1)} %all-reduce.3.cloned.1.call-done), kind=kLoop, calls=%fused_computation.9 | loop fusion | flops 2359295 | bytes 1572868 | tf_op jit(solution)/shard_map/reduce_sum | solution.py:53
  84.2 5.5 %psum.29 = f32[]{:T(128)} all-reduce(f32[]{:T(128)} %fusion.1), channel_id=1, replica_groups=mesh['ctx'=2,'tok'=8,'head'=2] {'head'}, use_global_device_ids=true, to_apply=%region_2.0 | all-reduce | flops 1 | bytes 8 | tf_op jit(solution)/shard_map/psum | solution.py:53
  90.5 2.3 fusion
  92.8 1.8 divide_convert_fusion.1
  94.7 4.6 %collective-permute-start = (bf16[2,3,256,512]{3,2,0,1:T(8,128)(2,1)}, bf16[2,3,256,512]{3,2,0,1:T(8,128)(2,1)}, u32[]{:S(2)}, u32[]{:S(2)}) collective-permute-start(bf16[2,3,256,512]{3,2,0,1:T(8,128)(2,1)} %divide_convert_fusion.1), channel_id=1, source_target_pairs={{0,16},{1,17},{2,18},{3,19},{4,20},{5,21},{6,22},{7,23},{8,24},{9,... | collective-permute-start | bytes 4718600 | tf_op jit(solution)/shard_map/ppermute | solution.py:10
  99.3 30.1 %collective-permute-done = bf16[2,3,256,512]{3,2,0,1:T(8,128)(2,1)} collective-permute-done((bf16[2,3,256,512]{3,2,0,1:T(8,128)(2,1)}, bf16[2,3,256,512]{3,2,0,1:T(8,128)(2,1)}, u32[]{:S(2)}, u32[]{:S(2)}) %collective-permute-start) | collective-permute-done | bytes 1572896 | tf_op jit(solution)/shard_map/ppermute | solution.py:10
  129.4 1.6 copy_select_fusion
  132.2 0.8 copy-done.7
  133.0 0.6 fusion.94
  133.6 1.4 fusion.60
  135.1 1.5 fusion.53
  136.6 1.2 fusion.57
  137.8 1.3 maximum_bitcast_fusion.1
  139.2 0.6 copy-done.8
  139.8 3.3 %fusion.74 = f32[2,512,768]{1,2,0:T(8,128)} fusion(bf16[2,1,2,768,256]{4,3,2,1,0:T(8,128)(2,1)S(1)} %copy-done.8, bf16[2,3,256,512]{3,2,0,1:T(8,128)(2,1)} %divide_convert_fusion.1), kind=kOutput, calls=%fused_computation.92 | convolution fusion | flops 402653184 | bytes 4456448 | tf_op jit(solution)/shard_map/vmap()/dot_general | solution.py:30
  143.1 59.2 %all-reduce.5.cloned.1.call-done = bf16[2,3,256,512]{3,2,0,1:T(8,128)(2,1)} async-done(((bf16[2,3,256,512]{3,2,0,1:T(8,128)(2,1)}), bf16[2,3,256,512]{3,2,0,1:T(8,128)(2,1)}) %all-reduce.5.cloned.1.call-update) | async-done | bytes 1572880 | tf_op jit(solution)/shard_map/psum | solution.py:52
  202.2 2.8 %fusion.3 = f32[]{:T(128)} fusion(bf16[2,3,256,512]{3,2,0,1:T(8,128)(2,1)} %all-reduce.5.cloned.1.call-done), kind=kLoop, calls=%fused_computation.11 | loop fusion | flops 2359295 | bytes 1572868 | tf_op jit(solution)/shard_map/reduce_sum | solution.py:53
  205.0 4.7 %fusion.46 = bf16[1,2,768,256]{3,2,1,0:T(8,128)(2,1)} fusion(f32[2,512,768]{1,2,0:T(8,128)} %fusion.74, bf16[2,1,2,768,256]{4,3,2,1,0:T(8,128)(2,1)} %param.8, bf16[2,3,256,512]{3,2,0,1:T(8,128)(2,1)} %divide_convert_fusion.1), kind=kOutput, calls=%fused_computation.73 | convolution fusion | flops 810418176 | bytes 5767168 | tf_op jit(solution)/shard_map/vmap()/dot_general | solution.py:34
  209.7 5.5 %psum.31 = f32[]{:T(128)} all-reduce(f32[]{:T(128)} %fusion.3), channel_id=1, replica_groups=mesh['ctx'=2,'tok'=8,'head'=2] {'head'}, use_global_device_ids=true, to_apply=%region_7.8 | all-reduce | flops 1 | bytes 8 | tf_op jit(solution)/shard_map/psum | solution.py:53
  216.0 0.9 fusion.2
  216.9 0.7 divide_convert_fusion
  217.6 1.1 copy-done.5
  219.3 3.6 %fusion.47 = bf16[1,2,768,256]{3,2,1,0:T(8,128)(2,1)} fusion(f32[2,512,768]{1,2,0:T(8,128)S(1)} %fusion.64, bf16[2,1,2,768,256]{4,3,2,1,0:T(8,128)(2,1)} %param.8, bf16[2,3,256,512]{3,2,0,1:T(8,128)(2,1)} %copy-done.5), kind=kOutput, calls=%fused_computation.74 | convolution fusion | flops 810418176 | bytes 5767168 | tf_op jit(solution)/shard_map/vmap()/dot_general | solution.py:34
  222.9 2.7 %maximum_bitcast_fusion.2 = bf16[2,1,2,768,256]{4,3,2,1,0:T(8,128)(2,1)} fusion(bf16[1,2,768,256]{3,2,1,0:T(8,128)(2,1)} %fusion.47, bf16[1,2,768,256]{3,2,1,0:T(8,128)(2,1)} %fusion.46), kind=kLoop, calls=%fused_computation.52 | loop fusion | flops 786432 | bytes 3145728 | tf_op jit(solution)/shard_map/broadcast_in_dim | solution.py:68
  (32 shorter events, 3.4 us)
Async XLA Ops:
  6.5 1.9 copy-start.3
  6.5 74.8 %all-reduce.3.cloned.1.call-start = ((), (), s32[]{:S(2)}) async-start(), calls=%async_computation | async-start | bytes 3145728 | tf_op jit(solution)/shard_map/psum | solution.py:52
  9.0 0.7 copy-start.10
  9.0 1.4 copy-start.6
  15.2 75.2 %copy-start = (bf16[1,2,3,256,512]{4,3,2,1,0:T(8,128)(2,1)S(1)}, bf16[1,2,3,256,512]{4,3,2,1,0:T(8,128)(2,1)}, u32[]{:S(2)}) copy-start(bf16[1,2,3,256,512]{4,3,2,1,0:T(8,128)(2,1)} %param.10) | copy-start | bytes 4718596
  16.6 185.7 %all-reduce.5.cloned.1.call-start = ((), (), s32[]{:S(2)}) async-start(), calls=%async_computation.1 | async-start | bytes 3145728 | tf_op jit(solution)/shard_map/psum | solution.py:52
  81.3 11.5 %copy-start.2 = (bf16[2,3,256,512]{3,2,0,1:T(8,128)(2,1)S(1)}, bf16[2,3,256,512]{3,2,0,1:T(8,128)(2,1)}, u32[]{:S(2)}) copy-start(bf16[2,3,256,512]{3,2,0,1:T(8,128)(2,1)} %all-reduce.3.cloned.1.call-done) | copy-start | bytes 4718596
  94.7 36.4 %copy-start.4 = (bf16[2,1,2,768,256]{4,3,2,1,0:T(8,128)(2,1)S(1)}, bf16[2,1,2,768,256]{4,3,2,1,0:T(8,128)(2,1)}, u32[]{:S(2)}) copy-start(bf16[2,1,2,768,256]{4,3,2,1,0:T(8,128)(2,1)} %param.6) | copy-start | bytes 4718596
  94.7 34.8 %collective-permute-start = (bf16[2,3,256,512]{3,2,0,1:T(8,128)(2,1)}, bf16[2,3,256,512]{3,2,0,1:T(8,128)(2,1)}, u32[]{:S(2)}, u32[]{:S(2)}) collective-permute-start(bf16[2,3,256,512]{3,2,0,1:T(8,128)(2,1)} %divide_convert_fusion.1), channel_id=1, source_target_pairs={{0,16},{1,17},{2,18},{3,19},{4,20},{5,21},{6,22},{7,23},{8,24},{9,... | collective-permute-start | bytes 4718600 | tf_op jit(solution)/shard_map/ppermute | solution.py:10
  131.6 1.4 copy-start.7
  137.8 2.0 copy-start.8
  205.0 10.9 %copy-start.1 = (bf16[2,3,256,512]{3,2,0,1:T(8,128)(2,1)S(1)}, bf16[2,3,256,512]{3,2,0,1:T(8,128)(2,1)}, u32[]{:S(2)}) copy-start(bf16[2,3,256,512]{3,2,0,1:T(8,128)(2,1)} %all-reduce.5.cloned.1.call-done) | copy-start | bytes 4718596
  216.9 1.9 copy-start.9
  217.6 1.1 copy-start.5
Sparse Core Ops, SparseCore 0:
  16.7 64.5 all-reduce.2
  139.3 62.8 all-reduce.4
where the time goes:
time: 233 us; the launch traced here: 232 us
  waiting for transfers between devices  154 us (66%)
  matrix products  24.1 us (10%)
  other arithmetic  18.3 us (8%)
  between operations  15 us (6%)
  blocking collectives  11.1 us (5%)
  local copies, waits for them, and re-layouts  5.34 us (2%)
  starting transfers between devices  4.68 us (2%)
    psum x2, waiting for transfers between devices, block_tick(): summed = lax.psum(grads.astype(jnp.bfloat16), 'tok').astype(jnp.float32)  124 us
    ppermute x1, waiting for transfers between devices, from_behind(): lax.ppermute(value, axis, [(source, source + steps) for source in range(f...  30.1 us
    psum x2, blocking collectives, block_tick(): total_sq = lax.psum(jnp.sum(summed * summed), 'head')  11.1 us
    dot_general x2, matrix products, apply_state(): lax.dot_general(mixed, state[2], contract, preferred_element_type=jnp.flo...  8.33 us
    reduce_sum x2, other arithmetic, block_tick(): total_sq = lax.psum(jnp.sum(summed * summed), 'head')  5.73 us
    unnamed x23, local copies, waits for them, and re-layouts  5.3 us
  transfers between devices with their start and end apart: 3, of which 3 were waited for; matrix products, arithmetic and copies ran while one was open for 1% of the time, Pallas kernels for 0%

commit v1 on v0

v1 whole, which is shorter than its diff:
```python
import functools

import jax
import jax.numpy as jnp
from jax import lax
from jax.experimental import pallas as pl
from jax.experimental.pallas import tpu as pltpu
from jax.sharding import PartitionSpec as P

BF16 = jnp.bfloat16
F32 = jnp.float32
VMEM = pl.BlockSpec(memory_space=pltpu.VMEM)
SMEM = pl.BlockSpec(memory_space=pltpu.SMEM)


def matmul(a, b, contract=((1,), (0,))):
    return lax.dot_general(a, b, (contract, ((), ())), preferred_element_type=F32)


def sigmoid(x):
    return 0.5 * jnp.tanh(0.5 * x) + 0.5


def add_grads(state, pairs, acc, wide):
    hidden = state.shape[2]
    for index, (keys, weighted) in enumerate(pairs):
        for lo in range(0, hidden, wide):
            cols = slice(lo, lo + wide)
            h_one = matmul(keys, state[0, :, cols])
            h_three = matmul(keys, state[1, :, cols])
            dact = matmul(weighted, state[2, :, cols])
            sig = sigmoid(h_one)
            gated = h_one * sig
            act = (gated * h_three).astype(BF16)
            d_three = (dact * gated).astype(BF16)
            d_one = (dact * h_three * (sig + gated - gated * sig)).astype(BF16)
            for m, (left, right) in enumerate(((keys, d_one), (keys, d_three), (weighted, act))):
                part = matmul(left, right, ((0,), (0,)))
                if index == 0:
                    acc[m, :, cols] = part
                else:
                    acc[m, :, cols] += part


def put_shards(acc, row, outs):
    rows = outs[0].shape[1]
    for d, out in enumerate(outs):
        start = pl.multiple_of((row ^ d) * rows, rows)
        for m in range(acc.shape[0]):
            out[m] = acc[m, pl.ds(start, rows), :].astype(BF16)


def renorm(older, shards, row, total_sq, factor, moved, newer):
    rows = shards[0].shape[1]
    scale = factor * lax.rsqrt(total_sq[0:1, 0:1] + 1e-06)
    for m in range(older.shape[0]):
        old_sq = 0.0
        new_sq = 0.0
        for d, shard in enumerate(shards):
            start = pl.multiple_of((row ^ d) * rows, rows)
            old = older[m, pl.ds(start, rows), :].astype(F32)
            new = old + scale * shard[m].astype(F32)
            moved[pl.ds(start, rows), :] = new
            old_sq = old_sq + jnp.sum(old * old, axis=0, keepdims=True)
            new_sq = new_sq + jnp.sum(new * new, axis=0, keepdims=True)
        ratio = jnp.sqrt(old_sq) * lax.rsqrt(new_sq + 1e-06)
        newer[m] = (moved[...] * ratio).astype(BF16)


def applied(state, queries):
    p_one = matmul(queries, state[0])
    p_three = matmul(queries, state[1])
    mixed = (p_one * sigmoid(p_one) * p_three).astype(BF16)
    return matmul(mixed, state[2], ((1,), (1,))).astype(BF16)


def call(body, name, outs, specs, scratch, *args):
    return pl.pallas_call(
        body,
        out_shape=outs,
        in_specs=specs,
        out_specs=jax.tree.map(lambda _: VMEM, outs),
        scratch_shapes=scratch,
        name=name,
    )(*args)


def shape(*dims, dtype=BF16):
    return jax.ShapeDtypeStruct(dims, dtype)


def first_grads(where, state, mine, others, weighted, weighted_others):
    _, dims, hidden = state.shape
    count = lax.axis_size("tok") // 2
    outs = [shape(3, dims // count, hidden) for _ in range(count)]

    def body(where, state, mine, weighted, others, weighted_others, *rest):
        outs, acc = rest[:count], rest[count]
        pairs = [(mine[...], weighted[...]), (others[...], weighted_others[...])]
        add_grads(state, pairs, acc, 256)
        put_shards(acc, where[0], outs)

    return call(
        body, "first_grads", outs, [SMEM] + [VMEM] * 5, [pltpu.VMEM((3, dims, hidden), F32)],
        where, state, mine, weighted, others, weighted_others,
    )


def next_grads(where, older, shards, total_sq, factor, fresh, mine, others, weighted, weighted_others):
    _, dims, hidden = older.shape
    count = len(shards)
    outs = [shape(3, dims, hidden)] + [shape(3, dims // count, hidden) for _ in range(count)]

    def body(where, older, total_sq, fresh, mine, weighted, others, weighted_others, *rest):
        shards, newer, outs = rest[:count], rest[count], rest[count + 1 : 2 * count + 1]
        moved, state, acc = rest[2 * count + 1 :]
        renorm(older, shards, where[0], total_sq, factor, moved, newer)

        @pl.when(where[1] == 0)
        def _():
            state[...] = fresh[...]

        @pl.when(where[1] != 0)
        def _():
            state[...] = newer[...]

        pairs = [(mine[...], weighted[...]), (others[...], weighted_others[...])]
        add_grads(state, pairs, acc, 256)
        put_shards(acc, where[0], outs)

    scratch = [
        pltpu.VMEM((dims, hidden), F32), pltpu.VMEM((3, dims, hidden), BF16), pltpu.VMEM((3, dims, hidden), F32),
    ]
    got = call(
        body, "next_grads", outs, [SMEM] + [VMEM] * (7 + count), scratch,
        where, older, total_sq, fresh, mine, weighted, others, weighted_others, *shards,
    )
    return got[0], got[1:]


def shard_sum(parts):
    def body(*refs):
        parts, (out, square) = refs[:-2], refs[-2:]
        total_sq = 0.0
        for m in range(out.shape[0]):
            total = parts[0][m].astype(F32)
            for part in parts[1:]:
                total = total + part[m].astype(F32)
            out[m] = total.astype(BF16)
            total_sq = total_sq + jnp.sum(total * total, axis=(0, 1), keepdims=True)
        square[...] = jnp.broadcast_to(total_sq, square.shape)

    outs = [shape(*parts[0].shape), shape(8, 128, dtype=F32)]
    return call(body, "shard_sum", outs, [VMEM] * len(parts), [], *parts)


def apply_old(state, mine, others):
    def body(state, mine, others, out, out_others):
        out_others[...] = applied(state, others[...])
        out[...] = applied(state, mine[...])

    outs = [shape(*mine.shape), shape(*mine.shape)]
    return call(body, "apply_old", outs, [VMEM] * 3, [], state, mine, others)


def apply_new(where, older, shards, total_sq, factor, mine, others):
    _, dims, hidden = older.shape
    count = len(shards)

    def body(where, older, total_sq, mine, others, *rest):
        shards, out, out_others, moved, newer = rest[:count], *rest[count:]
        renorm(older, shards, where[0], total_sq, factor, moved, newer)
        out_others[...] = applied(newer, others[...])
        out[...] = applied(newer, mine[...])

    outs = [shape(*mine.shape), shape(*mine.shape)]
    scratch = [pltpu.VMEM((dims, hidden), F32), pltpu.VMEM((3, dims, hidden), BF16)]
    return call(
        body, "apply_new", outs, [SMEM] + [VMEM] * (4 + count), scratch,
        where, older, total_sq, mine, others, *shards,
    )


def after(value, *others):
    return lax.optimization_barrier((value, *others))[0]


def total_over(square, axis, step):
    while step < lax.axis_size(axis):
        pairs = [(i, i ^ step) for i in range(lax.axis_size(axis))]
        square = square + lax.ppermute(square, axis, pairs)
        step *= 2
    return square


def shards(keys, values, queries, rates, state_in, fresh):
    blocks, tok = lax.axis_size("ctx"), lax.axis_size("tok")
    heads_all = lax.axis_size("head") * state_in.shape[1]
    hidden = state_in.shape[-1]
    count = tok // 2
    assert state_in.shape[1] == 2 and tok == 2 * count and count & (count - 1) == 0
    factor = 0.5 * float(3 * hidden * heads_all) ** 0.5
    core = lax.axis_index("tok") % 2
    row = lax.axis_index("tok") // 2
    block = lax.axis_index("ctx")
    where = jnp.stack([row, block]).astype(jnp.int32)
    swap = [(i, i ^ 1) for i in range(tok)]
    forward = [(i, (i + 1) % blocks) for i in range(blocks)]
    backward = [(b, a) for a, b in forward]

    def along(d):
        return [(i, i ^ (2 * d)) for i in range(tok)]

    def across(d):
        return [(c * tok + a, (c + 1) % blocks * tok + b) for c in range(blocks) for a, b in along(d)]

    def both(array, tick):
        local = array[tick, 0]
        return (
            lax.dynamic_index_in_dim(local, core, 0, keepdims=False),
            lax.ppermute(lax.dynamic_index_in_dim(local, 1 - core, 0, keepdims=False), "tok", swap),
        )

    def mine(array):
        return lax.dynamic_index_in_dim(array, core, 0, keepdims=False)

    weighted = (rates[..., None] * values.astype(F32)).astype(BF16)
    state = mine(state_in[0])
    tokens = (*both(keys, 0), *both(weighted, 0))

    partial = first_grads(where, state, *tokens)
    later = after((keys[1:], weighted[1:], queries), partial[0])
    parts = [lax.ppermute(partial[d], ("ctx", "tok"), across(d)) for d in reversed(range(count))]
    next_tokens = (*both(later[0], 0), *both(later[1], 0))
    asks = [both(later[2], 0), both(later[2], 1)]
    shard, square = shard_sum(parts)
    older = lax.ppermute(after(state, shard), "ctx", forward)
    gathered = [shard] + [lax.ppermute(shard, "tok", along(d)) for d in range(1, count)]
    total_sq = total_over(total_over(square, "tok", 1), "head", 1)

    newer, partial = next_grads(where, older, gathered, total_sq, factor, mine(fresh), *next_tokens)
    incoming = jnp.where(block == 0, mine(fresh), newer)
    own = lax.ppermute(newer, "ctx", backward)
    parts = [partial[0]] + [lax.ppermute(partial[d], "tok", along(d)) for d in reversed(range(1, count))]
    shard, square = shard_sum(parts)
    gathered = [shard] + [lax.ppermute(shard, "tok", along(d)) for d in range(1, count)]
    total_sq = total_over(total_over(square, "tok", 1), "head", 1)
    early, early_others = apply_old(own, *asks[0])
    early_back = lax.ppermute(early_others, "tok", swap)
    late, late_others = apply_new(where, incoming, gathered, total_sq, factor, *asks[1])
    late_back = lax.ppermute(late_others, "tok", swap)

    def heads(own, other):
        return jnp.where(core == 0, jnp.stack([own, other]), jnp.stack([other, own]))

    return jnp.stack([heads(early, early_back), heads(late, late_back)])[:, None]


def solution(mesh):
    in_specs = (
        P(None, "ctx", "head", "tok", None),
        P(None, "ctx", "head", "tok", None),
        P(None, "ctx", "head", "tok", None),
        P(None, "ctx", "head", "tok"),
        P("ctx", "head", None, None, None),
        P("head", None, None, None),
    )
    out_specs = P(None, "ctx", "head", "tok", None)
    return jax.shard_map(shards, mesh=mesh, in_specs=in_specs, out_specs=out_specs, check_vma=False)
```

time: 233 us -> 155 us (0.67)
  waiting for transfers between devices: 154 us -> 66.1 us
  starting transfers between devices: 4.68 us -> 40.3 us
  Pallas kernels: 0 us -> 24.9 us
  matrix products: 24.1 us -> 0 us
  between operations: 15 us -> 0.23 us
  blocking collectives: 11.1 us -> 0 us
  other arithmetic: 18.3 us -> 8.78 us
  local copies, waits for them, and re-layouts: 5.34 us -> 14.7 us
    psum x2 -> x0, waiting for transfers between devices: 124 us -> none  [block_tick(): summed = lax.psum(grads.astype(jnp.bfloat16), 'tok').astype(jnp.float32)]
    ppermute x1 -> x31, waiting for transfers between devices: 30.1 us -> 66.1 us  [the longest x6 24.1 us: shards(): lax.ppermute(shard, 'tok', along(d))]
    ppermute x1 -> x31, starting transfers between devices: 4.64 us -> 40.3 us  [the longest x6 16.4 us: shards(): lax.ppermute(shard, 'tok', along(d))]
    pallas_call x0 -> x6, Pallas kernels: none -> 24.9 us  [call(): pl.pallas_call(body, out_shape=outs, in_specs=specs, out_specs=jax.tree.m...]
    dot_general x16 -> x0, matrix products: 24.1 us -> none  [the longest x2 8.33 us: apply_state(): lax.dot_general(mixed, state[2], contract, preferred_element_type=jnp.flo...]
    psum x2 -> x0, blocking collectives: 11.1 us -> none  [block_tick(): total_sq = lax.psum(jnp.sum(summed * summed), 'head')]
    reduce_sum x4 -> x0, other arithmetic: 8.88 us -> none  [the longest x2 5.73 us: block_tick(): total_sq = lax.psum(jnp.sum(summed * summed), 'head')]
    squeeze x0 -> x8, local copies, waits for them, and re-layouts: none -> 8.15 us  [the longest x6 6.25 us: both(): lax.dynamic_index_in_dim(local, 1 - core, 0, keepdims=False)]
  transfers between devices with their start and end apart: 3 -> 31, of which waited for: 3 -> 16; matrix products, arithmetic and copies ran while one was open for 1% -> 8% of each run, Pallas kernels for 0% -> 11%
where the time goes in v1:
time: 155 us
  waiting for transfers between devices  66.1 us (43%)
  starting transfers between devices  40.3 us (26%)
  Pallas kernels  24.9 us (16%)
  local copies, waits for them, and re-layouts  14.7 us (9%)
  other arithmetic  8.78 us (6%)
    pallas_call x6, Pallas kernels, call(): pl.pallas_call(body, out_shape=outs, in_specs=specs, out_specs=jax.tree.m...  24.9 us
    ppermute x6, waiting for transfers between devices, shards(): lax.ppermute(shard, 'tok', along(d))  24.1 us
    ppermute x4, waiting for transfers between devices, shards(): lax.ppermute(partial[d], ('ctx', 'tok'), across(d))  16.5 us
    ppermute x6, starting transfers between devices, shards(): lax.ppermute(shard, 'tok', along(d))  16.4 us
    ppermute x3, waiting for transfers between devices, shards(): lax.ppermute(partial[d], 'tok', along(d))  14 us
    ppermute x8, waiting for transfers between devices, total_over(): square = square + lax.ppermute(square, axis, pairs)  11.2 us
    ppermute x4, starting transfers between devices, shards(): lax.ppermute(partial[d], ('ctx', 'tok'), across(d))  7.58 us
    ppermute x8, starting transfers between devices, total_over(): square = square + lax.ppermute(square, axis, pairs)  7.35 us
  transfers between devices with their start and end apart: 31, of which 16 were waited for; matrix products, arithmetic and copies ran while one was open for 8% of the time, Pallas kernels for 11%

profile of v1, /device:TPU:0, one launch (start us, length us, event | category | flops | bytes accessed | tf_op | source)
XLA Modules:
  0.0 155.0 jit_solution(1521496741669979688)
XLA Ops:
  0.0 2.0 %multiply_convert_fusion = bf16[2,1,2,768,256]{4,3,2,1,0:T(8,128)(2,1)S(1)} fusion(bf16[2,1,2,768,256]{4,3,2,1,0:T(8,128)(2,1)} %param.7, f32[2,2,768]{2,1,0:T(2,128)} %bitcast.44), kind=kLoop, calls=%fused_computation | loop fusion | flops 2359296 | bytes 3158016 | tf_op jit(solution)/shard_map/convert_element_type | solution.py:227
  8.6 5.7 %first_grads.1 = (bf16[3,64,512]{2,1,0:T(8,128)(2,1)}, bf16[3,64,512]{2,1,0:T(8,128)(2,1)}, bf16[3,64,512]{2,1,0:T(8,128)(2,1)}, bf16[3,64,512]{2,1,0:T(8,128)(2,1)}) custom-call(s32[2]{0:T(128)} %pad_add_fusion.where, bf16[3,256,512]{2,1,0:T(8,128)(2,1)} %dynamic-slice_bitcast_fusion.1.state, bf16[768,256]{1,0:T(8,128)(2,1)} %get-tuple-element.64.mine, ...), custom_call_target="tpu_custom_call" | custom-call | tf_op jit(solution)/shard_map/first_grads/pallas_call | solution.py:78
  14.3 5.6 %collective-permute-start.2 = (bf16[3,64,512]{2,1,0:T(8,128)(2,1)}, bf16[3,64,512]{2,1,0:T(8,128)(2,1)S(1)}, u32[]{:S(2)}, u32[]{:S(2)}) collective-permute-start(bf16[3,64,512]{2,1,0:T(8,128)(2,1)} %get-tuple-element.26), channel_id=1, source_target_pairs={{0,28},{2,30},{4,24},{6,26},{8,20},{10,22},{12,16},{14,18},{16,12}... | collective-permute-start | bytes 589832 | tf_op jit(solution)/shard_map/ppermute | solution.py:233
  19.8 1.7 %collective-permute-start.4 = (bf16[3,64,512]{2,1,0:T(8,128)(2,1)}, bf16[3,64,512]{2,1,0:T(8,128)(2,1)}, u32[]{:S(2)}, u32[]{:S(2)}) collective-permute-start(bf16[3,64,512]{2,1,0:T(8,128)(2,1)} %get-tuple-element.28), channel_id=1, source_target_pairs={{0,20},{2,22},{4,16},{6,18},{8,28},{10,30},{12,24},{14,26},{16,4},... | collective-permute-start | bytes 589832 | tf_op jit(solution)/shard_map/ppermute | solution.py:233
  21.9 4.1 %collective-permute-done.2.refs_0_ = bf16[3,64,512]{2,1,0:T(8,128)(2,1)S(1)} collective-permute-done((bf16[3,64,512]{2,1,0:T(8,128)(2,1)}, bf16[3,64,512]{2,1,0:T(8,128)(2,1)S(1)}, u32[]{:S(2)}, u32[]{:S(2)}) %collective-permute-start.2) | collective-permute-done | bytes 196640 | tf_op jit(solution)/shard_map/ppermute | solution.py:233
  26.0 12.3 %collective-permute-done.3.refs_1_ = bf16[3,64,512]{2,1,0:T(8,128)(2,1)S(1)} collective-permute-done((bf16[3,64,512]{2,1,0:T(8,128)(2,1)}, bf16[3,64,512]{2,1,0:T(8,128)(2,1)S(1)}, u32[]{:S(2)}, u32[]{:S(2)}) %collective-permute-start.3) | collective-permute-done | bytes 196640 | tf_op jit(solution)/shard_map/ppermute | solution.py:233
  39.0 2.1 %shard_sum.2 = (bf16[3,64,512]{2,1,0:T(8,128)(2,1)}, f32[8,128]{1,0:T(8,128)}) custom-call(bf16[3,64,512]{2,1,0:T(8,128)(2,1)} %copy-done.19, bf16[3,64,512]{2,1,0:T(8,128)(2,1)} %copy-done.20, bf16[3,64,512]{2,1,0:T(8,128)(2,1)} %collective-permute-done.4.refs_2_, bf16[3,64,512]{2,1,0:T(8,128)(2,1)} %collective-permute-done.5.refs_3_), custom_call_target="tpu_custom_call" | custom-call | tf_op jit(solution)/shard_map/shard_sum/pallas_call | solution.py:78
  41.1 1.4 collective-permute-done.7
  43.1 1.8 %collective-permute-start.8 = (f32[8,128]{1,0:T(8,128)S(1)}, f32[8,128]{1,0:T(8,128)S(1)}, u32[]{:S(2)}, u32[]{:S(2)}) collective-permute-start(f32[8,128]{1,0:T(8,128)S(1)} %add.54), channel_id=1, source_target_pairs={{0,4},{2,6},{4,0},{6,2},{8,12},{10,14},{12,8},{14,10},{1,5},{3,7},... | collective-permute-start | bytes 12296 | tf_op jit(solution)/shard_map/ppermute | solution.py:191
  46.8 3.0 %collective-permute-start.9 = (f32[8,128]{1,0:T(8,128)S(1)}, f32[8,128]{1,0:T(8,128)S(1)}, u32[]{:S(2)}, u32[]{:S(2)}) collective-permute-start(f32[8,128]{1,0:T(8,128)S(1)} %add.55), channel_id=1, source_target_pairs={{0,8},{2,10},{4,12},{6,14},{8,0},{10,2},{12,4},{14,6},{1,9},{3,11}... | collective-permute-start | bytes 12296 | tf_op jit(solution)/shard_map/ppermute | solution.py:191
  49.7 1.9 %dynamic-slice_bitcast_fusion.7 = (bf16[768,256]{1,0:T(8,128)(2,1)S(1)}, bf16[768,256]{1,0:T(8,128)(2,1)}) fusion(bf16[1,1,2,768,256]{4,3,2,1,0:T(8,128)(2,1)} %get-tuple-element.33, s32[]{:T(128)S(6)} %select_n.70, s32[]{:T(128)S(6)} %select_n.69), kind=kLoop, calls=%fused_computation.12 | loop fusion | bytes 1572872 | tf_op jit(solution)/shard_map/jit(dynamic_index_in_dim)/squeeze | solution.py:221
  51.7 1.6 %collective-permute-start.10 = (f32[8,128]{1,0:T(8,128)S(1)}, f32[8,128]{1,0:T(8,128)S(1)}, u32[]{:S(2)}, u32[]{:S(2)}) collective-permute-start(f32[8,128]{1,0:T(8,128)S(1)} %add.56), channel_id=1, source_target_pairs={{0,1},{1,0},{2,3},{3,2},{4,5},{5,4},{6,7},{7,6},{8,9},{9,8},{10,11... | collective-permute-start | bytes 12296 | tf_op jit(solution)/shard_map/ppermute | solution.py:191
  54.2 3.8 %collective-permute-start.15 = (bf16[3,64,512]{2,1,0:T(8,128)(2,1)S(1)}, bf16[3,64,512]{2,1,0:T(8,128)(2,1)S(1)}, u32[]{:S(2)}, u32[]{:S(2)}) collective-permute-start(bf16[3,64,512]{2,1,0:T(8,128)(2,1)S(1)} %copy-done.15), channel_id=1, source_target_pairs={{0,12},{2,14},{4,8},{6,10},{8,4},{10,6},{12,0},{14,2},{1,13},{3,15... | collective-permute-start | bytes 589832 | tf_op jit(solution)/shard_map/ppermute | solution.py:238
  58.2 5.7 %collective-permute-done.15.rest_3_ = bf16[3,64,512]{2,1,0:T(8,128)(2,1)S(1)} collective-permute-done((bf16[3,64,512]{2,1,0:T(8,128)(2,1)S(1)}, bf16[3,64,512]{2,1,0:T(8,128)(2,1)S(1)}, u32[]{:S(2)}, u32[]{:S(2)}) %collective-permute-start.15) | collective-permute-done | bytes 196640 | tf_op jit(solution)/shard_map/ppermute | solution.py:238
  63.9 8.6 %collective-permute-start.13 = (bf16[3,64,512]{2,1,0:T(8,128)(2,1)S(1)}, bf16[3,64,512]{2,1,0:T(8,128)(2,1)S(1)}, u32[]{:S(2)}, u32[]{:S(2)}) collective-permute-start(bf16[3,64,512]{2,1,0:T(8,128)(2,1)S(1)} %copy-done.15), channel_id=1, source_target_pairs={{0,4},{2,6},{4,0},{6,2},{8,12},{10,14},{12,8},{14,10},{1,5},{3,7},... | collective-permute-start | bytes 589832 | tf_op jit(solution)/shard_map/ppermute | solution.py:238
  73.4 2.2 %collective-permute-done.14.rest_2_ = bf16[3,64,512]{2,1,0:T(8,128)(2,1)S(1)} collective-permute-done((bf16[3,64,512]{2,1,0:T(8,128)(2,1)S(1)}, bf16[3,64,512]{2,1,0:T(8,128)(2,1)S(1)}, u32[]{:S(2)}, u32[]{:S(2)}) %collective-permute-start.14) | collective-permute-done | bytes 196640 | tf_op jit(solution)/shard_map/ppermute | solution.py:238
  77.2 2.5 %collective-permute-done.13.rest_1_ = bf16[3,64,512]{2,1,0:T(8,128)(2,1)S(1)} collective-permute-done((bf16[3,64,512]{2,1,0:T(8,128)(2,1)S(1)}, bf16[3,64,512]{2,1,0:T(8,128)(2,1)S(1)}, u32[]{:S(2)}, u32[]{:S(2)}) %collective-permute-start.13) | collective-permute-done | bytes 196640 | tf_op jit(solution)/shard_map/ppermute | solution.py:238
  81.0 7.0 %next_grads.1 = (bf16[3,256,512]{2,1,0:T(8,128)(2,1)}, bf16[3,64,512]{2,1,0:T(8,128)(2,1)}, bf16[3,64,512]{2,1,0:T(8,128)(2,1)}, bf16[3,64,512]{2,1,0:T(8,128)(2,1)}, bf16[3,64,512]{2,1,0:T(8,128)(2,1)}) custom-call(s32[2]{0:T(128)} %pad_add_fusion.where, bf16[3,256,512]{2,1,0:T(8,128)(2,1)} %copy-done.6, f32[8,128]{1,0:T(8,128)} %add.57.total_sq, ...), custom_call_target="tpu_custom_call" | custom-call | tf_op jit(solution)/shard_map/next_grads/pallas_call | solution.py:78
  88.0 1.5 collective-permute-start.16
  89.5 2.0 %collective-permute-start.19 = (bf16[3,64,512]{2,1,0:T(8,128)(2,1)}, bf16[3,64,512]{2,1,0:T(8,128)(2,1)S(1)}, u32[]{:S(2)}, u32[]{:S(2)}) collective-permute-start(bf16[3,64,512]{2,1,0:T(8,128)(2,1)} %get-tuple-element.40), channel_id=1, source_target_pairs={{0,12},{2,14},{4,8},{6,10},{8,4},{10,6},{12,0},{14,2},{1,13},{3,15... | collective-permute-start | bytes 589832 | tf_op jit(solution)/shard_map/ppermute | solution.py:244
  91.5 2.4 %collective-permute-start.21 = (bf16[3,64,512]{2,1,0:T(8,128)(2,1)}, bf16[3,64,512]{2,1,0:T(8,128)(2,1)}, u32[]{:S(2)}, u32[]{:S(2)}) collective-permute-start(bf16[3,64,512]{2,1,0:T(8,128)(2,1)} %get-tuple-element.42), channel_id=1, source_target_pairs={{0,4},{2,6},{4,0},{6,2},{8,12},{10,14},{12,8},{14,10},{1,5},{3,7},... | collective-permute-start | bytes 589832 | tf_op jit(solution)/shard_map/ppermute | solution.py:244
  93.9 5.5 %collective-permute-done.19.refs_1_ = bf16[3,64,512]{2,1,0:T(8,128)(2,1)S(1)} collective-permute-done((bf16[3,64,512]{2,1,0:T(8,128)(2,1)}, bf16[3,64,512]{2,1,0:T(8,128)(2,1)S(1)}, u32[]{:S(2)}, u32[]{:S(2)}) %collective-permute-start.19) | collective-permute-done | bytes 196640 | tf_op jit(solution)/shard_map/ppermute | solution.py:244
  99.4 8.5 %collective-permute-done.20.refs_2_ = bf16[3,64,512]{2,1,0:T(8,128)(2,1)S(1)} collective-permute-done((bf16[3,64,512]{2,1,0:T(8,128)(2,1)}, bf16[3,64,512]{2,1,0:T(8,128)(2,1)S(1)}, u32[]{:S(2)}, u32[]{:S(2)}) %collective-permute-start.20) | collective-permute-done | bytes 196640 | tf_op jit(solution)/shard_map/ppermute | solution.py:244
  108.6 2.1 %shard_sum.3 = (bf16[3,64,512]{2,1,0:T(8,128)(2,1)}, f32[8,128]{1,0:T(8,128)}) custom-call(bf16[3,64,512]{2,1,0:T(8,128)(2,1)} %get-tuple-element.39.refs_0_, bf16[3,64,512]{2,1,0:T(8,128)(2,1)} %copy-done.21, bf16[3,64,512]{2,1,0:T(8,128)(2,1)} %copy-done.22, bf16[3,64,512]{2,1,0:T(8,128)(2,1)} %collective-permute-done.21.refs_3_), custom_call_target="tpu_custom_call" | custom-call | tf_op jit(solution)/shard_map/shard_sum/pallas_call | solution.py:78
  112.7 3.6 %collective-permute-done.23 = f32[8,128]{1,0:T(8,128)S(1)} collective-permute-done((f32[8,128]{1,0:T(8,128)S(1)}, f32[8,128]{1,0:T(8,128)S(1)}, u32[]{:S(2)}, u32[]{:S(2)}) %collective-permute-start.23) | collective-permute-done | bytes 4128 | tf_op jit(solution)/shard_map/ppermute | solution.py:191
  116.8 4.0 %collective-permute-done.24 = f32[8,128]{1,0:T(8,128)S(1)} collective-permute-done((f32[8,128]{1,0:T(8,128)S(1)}, f32[8,128]{1,0:T(8,128)S(1)}, u32[]{:S(2)}, u32[]{:S(2)}) %collective-permute-start.24) | collective-permute-done | bytes 4128 | tf_op jit(solution)/shard_map/ppermute | solution.py:191
  122.1 2.0 %collective-permute-start.29 = (bf16[3,64,512]{2,1,0:T(8,128)(2,1)}, bf16[3,64,512]{2,1,0:T(8,128)(2,1)S(1)}, u32[]{:S(2)}, u32[]{:S(2)}) collective-permute-start(bf16[3,64,512]{2,1,0:T(8,128)(2,1)} %get-tuple-element.44.rest_0_), channel_id=1, source_target_pairs={{0,12},{2,14},{4,8},{6,10},{8,4},{10,6},{12,0},{14,2},{1,13},{3,15... | collective-permute-start | bytes 589832 | tf_op jit(solution)/shard_map/ppermute | solution.py:246
  124.4 2.1 %collective-permute-start.27 = (bf16[3,64,512]{2,1,0:T(8,128)(2,1)}, bf16[3,64,512]{2,1,0:T(8,128)(2,1)}, u32[]{:S(2)}, u32[]{:S(2)}) collective-permute-start(bf16[3,64,512]{2,1,0:T(8,128)(2,1)} %get-tuple-element.44.rest_0_), channel_id=1, source_target_pairs={{0,4},{2,6},{4,0},{6,2},{8,12},{10,14},{12,8},{14,10},{1,5},{3,7},... | collective-permute-start | bytes 589832 | tf_op jit(solution)/shard_map/ppermute | solution.py:246
  128.1 4.0 %collective-permute-done.29.rest_3_ = bf16[3,64,512]{2,1,0:T(8,128)(2,1)S(1)} collective-permute-done((bf16[3,64,512]{2,1,0:T(8,128)(2,1)}, bf16[3,64,512]{2,1,0:T(8,128)(2,1)S(1)}, u32[]{:S(2)}, u32[]{:S(2)}) %collective-permute-start.29) | collective-permute-done | bytes 196640 | tf_op jit(solution)/shard_map/ppermute | solution.py:246
  132.0 9.7 %collective-permute-done.28.rest_2_ = bf16[3,64,512]{2,1,0:T(8,128)(2,1)S(1)} collective-permute-done((bf16[3,64,512]{2,1,0:T(8,128)(2,1)}, bf16[3,64,512]{2,1,0:T(8,128)(2,1)S(1)}, u32[]{:S(2)}, u32[]{:S(2)}) %collective-permute-start.28) | collective-permute-done | bytes 196640 | tf_op jit(solution)/shard_map/ppermute | solution.py:246
  142.4 4.5 %apply_new.1 = (bf16[768,256]{1,0:T(8,128)(2,1)}, bf16[768,256]{1,0:T(8,128)(2,1)}) custom-call(s32[2]{0:T(128)} %pad_add_fusion.where, bf16[3,256,512]{2,1,0:T(8,128)(2,1)} %broadcast_select_fusion.older, f32[8,128]{1,0:T(8,128)} %add.61.total_sq, bf16[768,256]{1,0:T(8,128)(2,1)} %get-tuple-element.56.mine, ...), custom_call_target="tpu_custom_call" | custom-call | tf_op jit(solution)/shard_map/apply_new/pallas_call | solution.py:78
  147.9 3.6 %apply_old.1 = (bf16[768,256]{1,0:T(8,128)(2,1)}, bf16[768,256]{1,0:T(8,128)(2,1)}) custom-call(bf16[3,256,512]{2,1,0:T(8,128)(2,1)} %copy-done.7, bf16[768,256]{1,0:T(8,128)(2,1)} %get-tuple-element.54.mine, bf16[768,256]{1,0:T(8,128)(2,1)} %copy-done.12), custom_call_target="tpu_custom_call" | custom-call | tf_op jit(solution)/shard_map/apply_old/pallas_call | solution.py:78
  (111 shorter events, 26.5 us)
Async XLA Ops:
  3.1 4.6 %collective-permute-start.1 = (bf16[768,256]{1,0:T(8,128)(2,1)}, bf16[768,256]{1,0:T(8,128)(2,1)S(1)}, u32[]{:S(2)}, u32[]{:S(2)}) collective-permute-start(bf16[768,256]{1,0:T(8,128)(2,1)} %get-tuple-element.61), channel_id=1, source_target_pairs={{0,2},{2,0},{4,6},{6,4},{8,10},{10,8},{12,14},{14,12},{1,3},{3,1},... | collective-permute-start | bytes 1179656 | tf_op jit(solution)/shard_map/ppermute | solution.py:221
  5.6 2.0 %collective-permute-start = (bf16[768,256]{1,0:T(8,128)(2,1)S(1)}, bf16[768,256]{1,0:T(8,128)(2,1)S(1)}, u32[]{:S(2)}, u32[]{:S(2)}) collective-permute-start(bf16[768,256]{1,0:T(8,128)(2,1)S(1)} %get-tuple-element.63), channel_id=1, source_target_pairs={{0,2},{2,0},{4,6},{6,4},{8,10},{10,8},{12,14},{14,12},{1,3},{3,1},... | collective-permute-start | bytes 1179656 | tf_op jit(solution)/shard_map/ppermute | solution.py:221
  8.6 36.3 %copy-start.1 = (bf16[3,256,512]{2,1,0:T(8,128)(2,1)S(1)}, bf16[3,256,512]{2,1,0:T(8,128)(2,1)}, u32[]{:S(2)}) copy-start(bf16[3,256,512]{2,1,0:T(8,128)(2,1)} %dynamic-slice_bitcast_fusion.1.state) | copy-start | bytes 2359300
  14.3 11.7 %collective-permute-start.2 = (bf16[3,64,512]{2,1,0:T(8,128)(2,1)}, bf16[3,64,512]{2,1,0:T(8,128)(2,1)S(1)}, u32[]{:S(2)}, u32[]{:S(2)}) collective-permute-start(bf16[3,64,512]{2,1,0:T(8,128)(2,1)} %get-tuple-element.26), channel_id=1, source_target_pairs={{0,28},{2,30},{4,24},{6,26},{8,20},{10,22},{12,16},{14,18},{16,12}... | collective-permute-start | bytes 589832 | tf_op jit(solution)/shard_map/ppermute | solution.py:233
  19.8 18.5 %collective-permute-start.3 = (bf16[3,64,512]{2,1,0:T(8,128)(2,1)}, bf16[3,64,512]{2,1,0:T(8,128)(2,1)S(1)}, u32[]{:S(2)}, u32[]{:S(2)}) collective-permute-start(bf16[3,64,512]{2,1,0:T(8,128)(2,1)} %get-tuple-element.27), channel_id=1, source_target_pairs={{0,24},{2,26},{4,28},{6,30},{8,16},{10,18},{12,20},{14,22},{16,8},... | collective-permute-start | bytes 589832 | tf_op jit(solution)/shard_map/ppermute | solution.py:233
  19.8 18.5 %collective-permute-start.4 = (bf16[3,64,512]{2,1,0:T(8,128)(2,1)}, bf16[3,64,512]{2,1,0:T(8,128)(2,1)}, u32[]{:S(2)}, u32[]{:S(2)}) collective-permute-start(bf16[3,64,512]{2,1,0:T(8,128)(2,1)} %get-tuple-element.28), channel_id=1, source_target_pairs={{0,20},{2,22},{4,16},{6,18},{8,28},{10,30},{12,24},{14,26},{16,4},... | collective-permute-start | bytes 589832 | tf_op jit(solution)/shard_map/ppermute | solution.py:233
  21.5 16.8 %collective-permute-start.5 = (bf16[3,64,512]{2,1,0:T(8,128)(2,1)}, bf16[3,64,512]{2,1,0:T(8,128)(2,1)}, u32[]{:S(2)}, u32[]{:S(2)}) collective-permute-start(bf16[3,64,512]{2,1,0:T(8,128)(2,1)} %get-tuple-element.29), channel_id=1, source_target_pairs={{0,16},{2,18},{4,20},{6,22},{8,24},{10,26},{12,28},{14,30},{16,0},... | collective-permute-start | bytes 589832 | tf_op jit(solution)/shard_map/ppermute | solution.py:233
  41.1 1.4 collective-permute-start.7
  43.1 3.6 %collective-permute-start.8 = (f32[8,128]{1,0:T(8,128)S(1)}, f32[8,128]{1,0:T(8,128)S(1)}, u32[]{:S(2)}, u32[]{:S(2)}) collective-permute-start(f32[8,128]{1,0:T(8,128)S(1)} %add.54), channel_id=1, source_target_pairs={{0,4},{2,6},{4,0},{6,2},{8,12},{10,14},{12,8},{14,10},{1,5},{3,7},... | collective-permute-start | bytes 12296 | tf_op jit(solution)/shard_map/ppermute | solution.py:191
  44.9 34.8 %collective-permute-start.6 = (bf16[3,256,512]{2,1,0:T(8,128)(2,1)S(1)}, bf16[3,256,512]{2,1,0:T(8,128)(2,1)S(1)}, u32[]{:S(2)}, u32[]{:S(2)}) collective-permute-start(bf16[3,256,512]{2,1,0:T(8,128)(2,1)S(1)} %copy-done.1), channel_id=1, source_target_pairs={{0,16},{16,0},{1,17},{17,1},{2,18},{18,2},{3,19},{19,3},{4,20},{20... | collective-permute-start | bytes 2359304 | tf_op jit(solution)/shard_map/ppermute | solution.py:237
  46.8 4.9 %collective-permute-start.9 = (f32[8,128]{1,0:T(8,128)S(1)}, f32[8,128]{1,0:T(8,128)S(1)}, u32[]{:S(2)}, u32[]{:S(2)}) collective-permute-start(f32[8,128]{1,0:T(8,128)S(1)} %add.55), channel_id=1, source_target_pairs={{0,8},{2,10},{4,12},{6,14},{8,0},{10,2},{12,4},{14,6},{1,9},{3,11}... | collective-permute-start | bytes 12296 | tf_op jit(solution)/shard_map/ppermute | solution.py:191
  51.7 28.1 %collective-permute-start.11 = (bf16[768,256]{1,0:T(8,128)(2,1)S(1)}, bf16[768,256]{1,0:T(8,128)(2,1)S(1)}, u32[]{:S(2)}, u32[]{:S(2)}) collective-permute-start(bf16[768,256]{1,0:T(8,128)(2,1)S(1)} %get-tuple-element.59), channel_id=1, source_target_pairs={{0,2},{2,0},{4,6},{6,4},{8,10},{10,8},{12,14},{14,12},{1,3},{3,1},... | collective-permute-start | bytes 1179656 | tf_op jit(solution)/shard_map/ppermute | solution.py:221
  51.7 6.4 %collective-permute-start.10 = (f32[8,128]{1,0:T(8,128)S(1)}, f32[8,128]{1,0:T(8,128)S(1)}, u32[]{:S(2)}, u32[]{:S(2)}) collective-permute-start(f32[8,128]{1,0:T(8,128)S(1)} %add.56), channel_id=1, source_target_pairs={{0,1},{1,0},{2,3},{3,2},{4,5},{5,4},{6,7},{7,6},{8,9},{9,8},{10,11... | collective-permute-start | bytes 12296 | tf_op jit(solution)/shard_map/ppermute | solution.py:191
  54.1 25.6 %collective-permute-start.12 = (bf16[768,256]{1,0:T(8,128)(2,1)S(1)}, bf16[768,256]{1,0:T(8,128)(2,1)S(1)}, u32[]{:S(2)}, u32[]{:S(2)}) collective-permute-start(bf16[768,256]{1,0:T(8,128)(2,1)S(1)} %get-tuple-element.57), channel_id=1, source_target_pairs={{0,2},{2,0},{4,6},{6,4},{8,10},{10,8},{12,14},{14,12},{1,3},{3,1},... | collective-permute-start | bytes 1179656 | tf_op jit(solution)/shard_map/ppermute | solution.py:221
  54.2 9.7 %collective-permute-start.15 = (bf16[3,64,512]{2,1,0:T(8,128)(2,1)S(1)}, bf16[3,64,512]{2,1,0:T(8,128)(2,1)S(1)}, u32[]{:S(2)}, u32[]{:S(2)}) collective-permute-start(bf16[3,64,512]{2,1,0:T(8,128)(2,1)S(1)} %copy-done.15), channel_id=1, source_target_pairs={{0,12},{2,14},{4,8},{6,10},{8,4},{10,6},{12,0},{14,2},{1,13},{3,15... | collective-permute-start | bytes 589832 | tf_op jit(solution)/shard_map/ppermute | solution.py:238
  58.1 17.5 %collective-permute-start.14 = (bf16[3,64,512]{2,1,0:T(8,128)(2,1)S(1)}, bf16[3,64,512]{2,1,0:T(8,128)(2,1)S(1)}, u32[]{:S(2)}, u32[]{:S(2)}) collective-permute-start(bf16[3,64,512]{2,1,0:T(8,128)(2,1)S(1)} %copy-done.15), channel_id=1, source_target_pairs={{0,8},{2,10},{4,12},{6,14},{8,0},{10,2},{12,4},{14,6},{1,9},{3,11}... | collective-permute-start | bytes 589832 | tf_op jit(solution)/shard_map/ppermute | solution.py:238
  63.9 15.8 %collective-permute-start.13 = (bf16[3,64,512]{2,1,0:T(8,128)(2,1)S(1)}, bf16[3,64,512]{2,1,0:T(8,128)(2,1)S(1)}, u32[]{:S(2)}, u32[]{:S(2)}) collective-permute-start(bf16[3,64,512]{2,1,0:T(8,128)(2,1)S(1)} %copy-done.15), channel_id=1, source_target_pairs={{0,4},{2,6},{4,0},{6,2},{8,12},{10,14},{12,8},{14,10},{1,5},{3,7},... | collective-permute-start | bytes 589832 | tf_op jit(solution)/shard_map/ppermute | solution.py:238
  75.6 48.5 %collective-permute-start.26 = (bf16[768,256]{1,0:T(8,128)(2,1)}, bf16[768,256]{1,0:T(8,128)(2,1)}, u32[]{:S(2)}, u32[]{:S(2)}) collective-permute-start(bf16[768,256]{1,0:T(8,128)(2,1)} %get-tuple-element.55), channel_id=1, source_target_pairs={{0,2},{2,0},{4,6},{6,4},{8,10},{10,8},{12,14},{14,12},{1,3},{3,1},... | collective-permute-start | bytes 1179656 | tf_op jit(solution)/shard_map/ppermute | solution.py:221
  88.0 58.9 %collective-permute-start.16 = (bf16[3,256,512]{2,1,0:T(8,128)(2,1)}, bf16[3,256,512]{2,1,0:T(8,128)(2,1)S(1)}, u32[]{:S(2)}, u32[]{:S(2)}) collective-permute-start(bf16[3,256,512]{2,1,0:T(8,128)(2,1)} %get-tuple-element.35), channel_id=1, source_target_pairs={{16,0},{0,16},{17,1},{1,17},{18,2},{2,18},{19,3},{3,19},{20,4},{4,... | collective-permute-start | bytes 2359304 | tf_op jit(solution)/shard_map/ppermute | solution.py:243
  89.5 9.9 %collective-permute-start.19 = (bf16[3,64,512]{2,1,0:T(8,128)(2,1)}, bf16[3,64,512]{2,1,0:T(8,128)(2,1)S(1)}, u32[]{:S(2)}, u32[]{:S(2)}) collective-permute-start(bf16[3,64,512]{2,1,0:T(8,128)(2,1)} %get-tuple-element.40), channel_id=1, source_target_pairs={{0,12},{2,14},{4,8},{6,10},{8,4},{10,6},{12,0},{14,2},{1,13},{3,15... | collective-permute-start | bytes 589832 | tf_op jit(solution)/shard_map/ppermute | solution.py:244
  91.5 16.4 %collective-permute-start.20 = (bf16[3,64,512]{2,1,0:T(8,128)(2,1)}, bf16[3,64,512]{2,1,0:T(8,128)(2,1)S(1)}, u32[]{:S(2)}, u32[]{:S(2)}) collective-permute-start(bf16[3,64,512]{2,1,0:T(8,128)(2,1)} %get-tuple-element.41), channel_id=1, source_target_pairs={{0,8},{2,10},{4,12},{6,14},{8,0},{10,2},{12,4},{14,6},{1,9},{3,11}... | collective-permute-start | bytes 589832 | tf_op jit(solution)/shard_map/ppermute | solution.py:244
  91.5 16.4 %collective-permute-start.21 = (bf16[3,64,512]{2,1,0:T(8,128)(2,1)}, bf16[3,64,512]{2,1,0:T(8,128)(2,1)}, u32[]{:S(2)}, u32[]{:S(2)}) collective-permute-start(bf16[3,64,512]{2,1,0:T(8,128)(2,1)} %get-tuple-element.42), channel_id=1, source_target_pairs={{0,4},{2,6},{4,0},{6,2},{8,12},{10,14},{12,8},{14,10},{1,5},{3,7},... | collective-permute-start | bytes 589832 | tf_op jit(solution)/shard_map/ppermute | solution.py:244
  110.6 1.4 collective-permute-start.22
  112.7 3.6 %collective-permute-start.23 = (f32[8,128]{1,0:T(8,128)S(1)}, f32[8,128]{1,0:T(8,128)S(1)}, u32[]{:S(2)}, u32[]{:S(2)}) collective-permute-start(f32[8,128]{1,0:T(8,128)S(1)} %add.58), channel_id=1, source_target_pairs={{0,4},{2,6},{4,0},{6,2},{8,12},{10,14},{12,8},{14,10},{1,5},{3,7},... | collective-permute-start | bytes 12296 | tf_op jit(solution)/shard_map/ppermute | solution.py:191
  116.3 4.5 %collective-permute-start.24 = (f32[8,128]{1,0:T(8,128)S(1)}, f32[8,128]{1,0:T(8,128)S(1)}, u32[]{:S(2)}, u32[]{:S(2)}) collective-permute-start(f32[8,128]{1,0:T(8,128)S(1)} %add.59), channel_id=1, source_target_pairs={{0,8},{2,10},{4,12},{6,14},{8,0},{10,2},{12,4},{14,6},{1,9},{3,11}... | collective-permute-start | bytes 12296 | tf_op jit(solution)/shard_map/ppermute | solution.py:191
  120.8 3.6 %collective-permute-start.25 = (f32[8,128]{1,0:T(8,128)S(1)}, f32[8,128]{1,0:T(8,128)S(1)}, u32[]{:S(2)}, u32[]{:S(2)}) collective-permute-start(f32[8,128]{1,0:T(8,128)S(1)} %add.60), channel_id=1, source_target_pairs={{0,1},{1,0},{2,3},{3,2},{4,5},{5,4},{6,7},{7,6},{8,9},{9,8},{10,11... | collective-permute-start | bytes 12296 | tf_op jit(solution)/shard_map/ppermute | solution.py:191
  122.1 24.8 %collective-permute-start.17 = (bf16[768,256]{1,0:T(8,128)(2,1)S(1)}, bf16[768,256]{1,0:T(8,128)(2,1)S(1)}, u32[]{:S(2)}, u32[]{:S(2)}) collective-permute-start(bf16[768,256]{1,0:T(8,128)(2,1)S(1)} %get-tuple-element.53), channel_id=1, source_target_pairs={{0,2},{2,0},{4,6},{6,4},{8,10},{10,8},{12,14},{14,12},{1,3},{3,1},... | collective-permute-start | bytes 1179656 | tf_op jit(solution)/shard_map/ppermute | solution.py:221
  122.1 9.9 %collective-permute-start.29 = (bf16[3,64,512]{2,1,0:T(8,128)(2,1)}, bf16[3,64,512]{2,1,0:T(8,128)(2,1)S(1)}, u32[]{:S(2)}, u32[]{:S(2)}) collective-permute-start(bf16[3,64,512]{2,1,0:T(8,128)(2,1)} %get-tuple-element.44.rest_0_), channel_id=1, source_target_pairs={{0,12},{2,14},{4,8},{6,10},{8,4},{10,6},{12,0},{14,2},{1,13},{3,15... | collective-permute-start | bytes 589832 | tf_op jit(solution)/shard_map/ppermute | solution.py:246
  124.1 17.6 %collective-permute-start.28 = (bf16[3,64,512]{2,1,0:T(8,128)(2,1)}, bf16[3,64,512]{2,1,0:T(8,128)(2,1)S(1)}, u32[]{:S(2)}, u32[]{:S(2)}) collective-permute-start(bf16[3,64,512]{2,1,0:T(8,128)(2,1)} %get-tuple-element.44.rest_0_), channel_id=1, source_target_pairs={{0,8},{2,10},{4,12},{6,14},{8,0},{10,2},{12,4},{14,6},{1,9},{3,11}... | collective-permute-start | bytes 589832 | tf_op jit(solution)/shard_map/ppermute | solution.py:246
  124.4 17.3 %collective-permute-start.27 = (bf16[3,64,512]{2,1,0:T(8,128)(2,1)}, bf16[3,64,512]{2,1,0:T(8,128)(2,1)}, u32[]{:S(2)}, u32[]{:S(2)}) collective-permute-start(bf16[3,64,512]{2,1,0:T(8,128)(2,1)} %get-tuple-element.44.rest_0_), channel_id=1, source_target_pairs={{0,4},{2,6},{4,0},{6,2},{8,12},{10,14},{12,8},{14,10},{1,5},{3,7},... | collective-permute-start | bytes 589832 | tf_op jit(solution)/shard_map/ppermute | solution.py:246
  146.9 5.1 %collective-permute-start.30 = (bf16[768,256]{1,0:T(8,128)(2,1)}, bf16[768,256]{1,0:T(8,128)(2,1)}, u32[]{:S(2)}, u32[]{:S(2)}) collective-permute-start(bf16[768,256]{1,0:T(8,128)(2,1)} %get-tuple-element.46), channel_id=1, source_target_pairs={{0,2},{2,0},{4,6},{6,4},{8,10},{10,8},{12,14},{14,12},{1,3},{3,1},... | collective-permute-start | bytes 1179656 | tf_op jit(solution)/shard_map/ppermute | solution.py:251
  151.5 2.1 %collective-permute-start.18 = (bf16[768,256]{1,0:T(8,128)(2,1)}, bf16[768,256]{1,0:T(8,128)(2,1)S(1)}, u32[]{:S(2)}, u32[]{:S(2)}) collective-permute-start(bf16[768,256]{1,0:T(8,128)(2,1)} %get-tuple-element.38), channel_id=1, source_target_pairs={{0,2},{2,0},{4,6},{6,4},{8,10},{10,8},{12,14},{14,12},{1,3},{3,1},... | collective-permute-start | bytes 1179656 | tf_op jit(solution)/shard_map/ppermute | solution.py:249
  (24 other events, 119.7 us)
